TPU v7x, 128 devices: a whole 4x4x4 slice. The times are simulated.
128 devices in a mesh: row: 16 (over x_hi, y, core), col: 8 (over z, x_lo).
Axes of the slice: x: 4 (x_hi: 2, x_lo: 2; x = x_hi * 2 + x_lo), y: 4, z: 4, core: 2. Of those that a mesh axis runs over, the one named last changes fastest.
Arguments:
- values: float32 [8192, 8192], P('row', 'col'), may hold values from 0 to 10, as said below
- pattern: int32 [64, 64], replicated, may hold values from 0 to 1, as said below
- pruning: int32 [64, 64], replicated, may hold values from 0 to 1, as said below
- owners: int32 [64], replicated, may hold values from 0 to 63, as said below
Outputs:
- expanded: float32 [8192, 8192], P('row', 'col')
Inputs may be any that keep to these rules, and one draw needn't show every extreme that they name: `values`: positive scores. `pattern`: every diagonal block is present. `pruning`: every diagonal block is kept. `owners`: A permutation of the 64 column blocks. Of the 8 column blocks of one index of col, at most 2 are stored at the column blocks of any one index of col, and exactly 2 at those of some index.
All inputs are finite; a program needn't handle non-finite values.
Results may differ from a plain program's by a relative error of at most 0.00065.
Values may be sent and summed in bfloat16 or wider, within the bound.
No kernel may reach another device: no remote copies, remote signals or barrier semaphores. Data moves between devices by JAX's collectives and lax.ppermute only.
A program may use at most 128 MiB of HBM per device.

v0:
```python
import jax
import jax.numpy as jnp
from jax import lax
from jax.sharding import PartitionSpec as P

BLK = 128


def expand_mask(tile, mask, blk):
    rows_in, cols_in = tile.shape
    shaped = tile.reshape(rows_in // blk, blk, cols_in // blk, blk)
    return (shaped * mask.astype(tile.dtype)[:, None, :, None]).reshape(rows_in, cols_in)


def ranks_of(destination):
    width = destination.shape[-1]
    earlier = jnp.arange(width)[:, None] < jnp.arange(width)[None, :]
    same_dest = destination[..., :, None] == destination[..., None, :]
    return jnp.sum(jnp.where(same_dest & earlier, 1, 0), axis=-2).astype(jnp.int32)


def pack_blocks(tile, owners, me_col, ncols, capacity, blk):
    rows_in, cols_in = tile.shape
    width = cols_in // blk
    my_owners = lax.dynamic_slice(owners, (me_col * width,), (width,))
    destination = my_owners // width
    rank = ranks_of(destination)
    slot_ids = jnp.arange(ncols * capacity)
    selector = (
        (destination[None, :] == (slot_ids // capacity)[:, None])
        & (rank[None, :] == (slot_ids % capacity)[:, None])
    ).astype(tile.dtype)
    column_blocks = tile.reshape(rows_in, width, blk)
    outgoing = jnp.einsum(
        "pk,rkb->prb",
        selector,
        column_blocks,
        preferred_element_type=jnp.float32,
        precision=lax.Precision.HIGHEST,
    )
    return outgoing


def unpack_blocks(arrived, owners, me_col, ncols, capacity):
    slot_count, rows_in, blk = arrived.shape
    width = owners.shape[0] // ncols
    table = owners.reshape(ncols, width)
    rank = ranks_of(table // width)
    wanted = me_col * width + jnp.arange(width)
    matches = table[None, :, :] == wanted[:, None, None]
    which_slot = rank[:, :, None] == jnp.arange(capacity)[None, None, :]
    selector = jnp.sum(jnp.where(matches[:, :, :, None] & which_slot[None], 1, 0), axis=2)
    selector = selector.reshape(width, ncols * capacity).astype(arrived.dtype)
    placed = jnp.einsum(
        "sp,prb->rsb",
        selector,
        arrived,
        preferred_element_type=jnp.float32,
        precision=lax.Precision.HIGHEST,
    )
    return placed.reshape(rows_in, width * blk)


def body(values, pattern, pruning, owners):
    rows_dev, cols_dev = values.shape
    blk = BLK
    row_blocks = rows_dev // blk
    col_blocks = cols_dev // blk
    ncols = lax.axis_size("col")
    capacity = max(2, (col_blocks + ncols - 1) // ncols)
    me_row = lax.axis_index("row")
    me_col = lax.axis_index("col")
    local_pattern = lax.dynamic_slice(
        pattern, (me_row * row_blocks, me_col * col_blocks), (row_blocks, col_blocks)
    )
    masked = expand_mask(values, local_pattern, blk)
    colsum_in = lax.psum(jnp.sum(masked, axis=0), "row")
    stochastic = (masked / colsum_in[None, :]).astype(jnp.bfloat16)
    row_panel = lax.all_gather(stochastic, "col", axis=1, tiled=True)
    nodes = row_panel.shape[1]
    pruning_rows = lax.dynamic_slice(
        pruning, (me_row * row_blocks, 0), (row_blocks, pruning.shape[1])
    )
    kept_mask = lax.dynamic_slice_in_dim(pruning_rows, me_col * col_blocks, col_blocks, 1)
    square = jnp.dot(
        row_panel,
        lax.all_gather(stochastic, "row", axis=0, tiled=True),
        preferred_element_type=jnp.float32,
    )
    inflated = expand_mask(square * square, kept_mask, blk)
    colsum_out = lax.psum(jnp.sum(inflated, axis=0), "row")
    normalized = jnp.float32(nodes) * inflated / colsum_out[None, :]
    arrived_out = lax.all_to_all(
        pack_blocks(normalized, owners, me_col, ncols, capacity, blk),
        "col",
        split_axis=0,
        concat_axis=0,
        tiled=True,
    )
    result = unpack_blocks(arrived_out, owners, me_col, ncols, capacity)
    return result


def solution(mesh):
    return jax.shard_map(
        body,
        mesh=mesh,
        in_specs=(P("row", "col"), P(), P(), P()),
        out_specs=P("row", "col"),
        check_vma=False,
    )
```

profile of v0, /device:TPU:0, one launch (start us, length us, event | category | flops | bytes accessed | tf_op | source)
XLA Modules:
  0.0 452.6 jit_solution(7957865634004855820)
XLA Ops:
  6.5 0.0 all-gather.3.cloned.1.call-start
  6.5 0.0 copy-start
  6.5 0.9 dynamic-slice_convert_fusion.1
  7.4 0.2 mul.43
  7.7 0.5 copy-done
  8.1 0.7 fusion.2
  8.8 38.2 %psum.14 = f32[1024]{0:T(1024)S(1)} all-reduce(f32[1024]{0:T(1024)S(1)} %fusion.2), channel_id=1, replica_groups=mesh['row'=16,'col'=8] {'row'}, use_global_device_ids=true, to_apply=%region_2.0 | all-reduce | flops 1024 | bytes 8192 | tf_op jit(solution)/shard_map/psum | solution.py:77
  47.0 3.2 divide_convert_fusion
  50.2 0.0 copy-start.1
  50.2 0.0 all-gather.3.cloned.1.call-update
  50.3 0.0 all-gather.5.cloned.1.call-start
  50.3 0.7 all-gather.5.cloned.1.call-update
  51.0 0.0 copy-done.1
  51.0 0.1 and_select_fusion.2
  51.1 0.8 dynamic-slice_convert_fusion
  51.9 0.1 select_reduce_fusion.2
  52.0 164.6 %all-gather.3.cloned.1.call-done = bf16[512,8192]{1,0:T(8,128)(2,1)} async-done(((bf16[512,1024]{1,0:T(8,128)(2,1)}), bf16[512,8192]{1,0:T(8,128)(2,1)}) %all-gather.3.cloned.1.call-update) | async-done | bytes 8388624 | tf_op jit(solution)/shard_map/all_gather | solution.py:79
  216.6 112.1 %all-gather.5.cloned.1.call-done = bf16[8192,1024]{1,0:T(8,128)(2,1)} async-done(((bf16[512,1024]{1,0:T(8,128)(2,1)}), bf16[8192,1024]{1,0:T(8,128)(2,1)}) %all-gather.5.cloned.1.call-update) | async-done | bytes 16777232 | tf_op jit(solution)/shard_map/all_gather | solution.py:87
  328.7 0.2 mul.47
  328.9 14.8 %fusion.14 = (f32[1024]{0:T(1024)S(1)}, f32[512,1024]{1,0:T(8,128)S(1)}) fusion(f32[64,8,8,128]{3,2,1,0:T(8,128)S(1)} %bitcast.34, bf16[512,8192]{1,0:T(8,128)(2,1)} %all-gather.3.cloned.1.call-done, bf16[8192,1024]{1,0:T(8,128)(2,1)} %all-gather.5.cloned.1.call-done), kind=kOutput, calls=%fused_computation.43 | convolution fusion | flops 8591506432 | bytes 29364224 | tf_op jit(solution)/shard_map/dot_general | solution.py:85
  343.7 33.8 %psum.15 = f32[1024]{0:T(1024)S(1)} all-reduce(f32[1024]{0:T(1024)S(1)} %get-tuple-element.5), channel_id=1, replica_groups=mesh['row'=16,'col'=8] {'row'}, use_global_device_ids=true, to_apply=%region_4.5 | all-reduce | flops 1024 | bytes 8192 | tf_op jit(solution)/shard_map/psum | solution.py:91
  377.6 0.3 divide_bitcast_fusion
  377.8 0.5 copy.21
  378.3 1.9 fusion.5
  380.2 3.3 copy.12
  383.5 5.3 %all-to-all-start = ((f32[16,512,128]{2,1,0:T(8,128)}), f32[16,512,128]{2,1,0:T(8,128)}, u32[]{:S(2)}, u32[]{:S(2)}) async-start(f32[16,512,128]{2,1,0:T(8,128)} %copy.12), calls=%async_computation | async-start | bytes 8388608 | tf_op jit(solution)/shard_map/all_to_all | solution.py:93
  388.8 0.1 eq.99
  388.9 0.1 select_reduce_fusion.1
  389.0 0.1 broadcast_compare_fusion
  389.1 0.4 select_reduce_fusion
  389.5 0.1 copy.14
  389.6 47.6 %all-to-all-done = f32[16,512,128]{2,1,0:T(8,128)} async-done(((f32[16,512,128]{2,1,0:T(8,128)}), f32[16,512,128]{2,1,0:T(8,128)}, u32[]{:S(2)}, u32[]{:S(2)}) %all-to-all-start) | async-done | bytes 4194336 | tf_op jit(solution)/shard_map/all_to_all | solution.py:93
  437.1 6.8 %fusion = f32[512,128,8]{1,2,0:T(8,128)S(1)} fusion(f32[8,16,1]{0,1,2:T(8,128)S(1)} %bitcast.35, f32[16,512,128]{2,1,0:T(8,128)} %all-to-all-done), kind=kOutput, calls=%fused_computation | convolution fusion | flops 100663296 | bytes 6291968 | tf_op jit(solution)/shard_map/sp,prb->rsb/dot_general | solution.py:54
  444.0 1.8 copy.33
  (6 shorter events, 0.0 us)
Async XLA Ops:
  6.5 210.1 %all-gather.3.cloned.1.call-start = ((), (), s32[]{:S(2)}) async-start(), calls=%async_computation.1 | async-start | bytes 9437184 | tf_op jit(solution)/shard_map/all_gather | solution.py:79
  6.5 1.6 copy-start
  50.2 0.8 copy-start.1
  50.3 278.4 %all-gather.5.cloned.1.call-start = ((), (), s32[]{:S(2)}) async-start(), calls=%async_computation.2 | async-start | bytes 17825792 | tf_op jit(solution)/shard_map/all_gather | solution.py:87
  383.5 53.7 %all-to-all-start = ((f32[16,512,128]{2,1,0:T(8,128)}), f32[16,512,128]{2,1,0:T(8,128)}, u32[]{:S(2)}, u32[]{:S(2)}) async-start(f32[16,512,128]{2,1,0:T(8,128)} %copy.12), calls=%async_computation | async-start | bytes 8388608 | tf_op jit(solution)/shard_map/all_to_all | solution.py:93
Sparse Core Ops, SparseCore 0:
  50.4 166.1 all-gather.2
  219.0 109.6 all-gather.4
where the time goes:
time: 453 us
  waiting for transfers between devices  325 us (72%)
  blocking collectives  72 us (16%)
  matrix products  23.5 us (5%)
  between operations  13.5 us (3%)
  other arithmetic  6.6 us (1%)
  local copies, waits for them, and re-layouts  6.55 us (1%)
  starting transfers between devices  5.38 us (1%)
    all_gather x1, waiting for transfers between devices, body(): row_panel = lax.all_gather(stochastic, 'col', axis=1, tiled=True)  165 us
    all_gather x1, waiting for transfers between devices, body(): lax.all_gather(stochastic, 'row', axis=0, tiled=True)  112 us
    all_to_all x1, waiting for transfers between devices, body(): lax.all_to_all(pack_blocks(normalized, owners, me_col, ncols, capacity, b...  47.6 us
    psum x1, blocking collectives, body(): colsum_in = lax.psum(jnp.sum(masked, axis=0), 'row')  38.2 us
    psum x1, blocking collectives, body(): colsum_out = lax.psum(jnp.sum(inflated, axis=0), 'row')  33.8 us
    dot_general x1, matrix products, body(): jnp.dot(row_panel, lax.all_gather(stochastic, 'row', axis=0, tiled=True),...  14.8 us
  transfers between devices with their start and end apart: 3, of which 3 were waited for; matrix products, arithmetic and copies ran while one was open for 0% of the time, Pallas kernels for 0%

commit v1 on v0

--- a/solution.py
+++ b/solution.py
@@ -76,7 +76,7 @@
     masked = expand_mask(values, local_pattern, blk)
     colsum_in = lax.psum(jnp.sum(masked, axis=0), "row")
     stochastic = (masked / colsum_in[None, :]).astype(jnp.bfloat16)
-    row_panel = lax.all_gather(stochastic, "col", axis=1, tiled=True)
+    row_panel = jnp.concatenate(lax.all_gather(stochastic, "col"), axis=1)
     nodes = row_panel.shape[1]
     pruning_rows = lax.dynamic_slice(
         pruning, (me_row * row_blocks, 0), (row_blocks, pruning.shape[1])

time: 453 us -> 453 us (level)
  local copies, waits for them, and re-layouts: 6.55 us -> 18 us
  waiting for transfers between devices: 325 us -> 314 us
    all_gather x1, waiting for transfers between devices: 112 us -> 101 us  [body(): lax.all_gather(stochastic, 'row', axis=0, tiled=True)]
    reshape x0 -> x1, local copies, waits for them, and re-layouts: none -> 11.4 us  [body(): row_panel = jnp.concatenate(lax.all_gather(stochastic, 'col'), axis=1)]
  transfers between devices with their start and end apart: 3 -> 3, of which waited for: 3 -> 3; matrix products, arithmetic and copies ran while one was open for 0% -> 3% of each run, Pallas kernels for 0% -> 0%
where the time goes in v1:
time: 453 us
  waiting for transfers between devices  314 us (69%)
  blocking collectives  72 us (16%)
  matrix products  23.6 us (5%)
  local copies, waits for them, and re-layouts  18 us (4%)
  between operations  13.5 us (3%)
  other arithmetic  6.6 us (1%)
  starting transfers between devices  5.38 us (1%)
    all_gather x1, waiting for transfers between devices, body(): row_panel = jnp.concatenate(lax.all_gather(stochastic, 'col'), axis=1)  165 us
    all_gather x1, waiting for transfers between devices, body(): lax.all_gather(stochastic, 'row', axis=0, tiled=True)  101 us
    all_to_all x1, waiting for transfers between devices, body(): lax.all_to_all(pack_blocks(normalized, owners, me_col, ncols, capacity, b...  47.6 us
    psum x1, blocking collectives, body(): colsum_in = lax.psum(jnp.sum(masked, axis=0), 'row')  38.2 us
    psum x1, blocking collectives, body(): colsum_out = lax.psum(jnp.sum(inflated, axis=0), 'row')  33.8 us
    dot_general x1, matrix products, body(): jnp.dot(row_panel, lax.all_gather(stochastic, 'row', axis=0, tiled=True),...  14.9 us
    reshape x1, local copies, waits for them, and re-layouts, body(): row_panel = jnp.concatenate(lax.all_gather(stochastic, 'col'), axis=1)  11.4 us
  transfers between devices with their start and end apart: 3, of which 3 were waited for; matrix products, arithmetic and copies ran while one was open for 3% of the time, Pallas kernels for 0%

profile of v1, /device:TPU:0, one launch (start us, length us, event | category | flops | bytes accessed | tf_op | source)
XLA Modules:
  0.0 452.7 jit_solution(555574985806275335)
XLA Ops:
  6.5 0.0 all-gather.6.cloned.1.call-start
  6.5 0.0 copy-start
  6.5 0.9 dynamic-slice_convert_fusion.1
  7.4 0.2 mul.43
  7.7 0.5 copy-done
  8.1 0.7 fusion.2
  8.8 38.2 %psum.14 = f32[1024]{0:T(1024)S(1)} all-reduce(f32[1024]{0:T(1024)S(1)} %fusion.2), channel_id=1, replica_groups=mesh['row'=16,'col'=8] {'row'}, use_global_device_ids=true, to_apply=%region_2.0 | all-reduce | flops 1024 | bytes 8192 | tf_op jit(solution)/shard_map/psum | solution.py:77
  47.0 3.2 divide_convert_fusion
  50.2 0.0 copy-start.1
  50.2 0.0 all-gather.6.cloned.1.call-update
  50.3 0.0 all-gather.4.cloned.1.call-start
  50.3 0.7 all-gather.4.cloned.1.call-update
  51.0 0.0 copy-done.1
  51.0 0.1 and_select_fusion.2
  51.1 0.8 dynamic-slice_convert_fusion
  51.9 0.1 select_reduce_fusion.2
  52.0 164.6 %all-gather.6.cloned.1.call-done = bf16[4096,1024]{1,0:T(8,128)(2,1)} async-done(((bf16[512,1024]{1,0:T(8,128)(2,1)}), bf16[4096,1024]{1,0:T(8,128)(2,1)}) %all-gather.6.cloned.1.call-update) | async-done | bytes 8388624 | tf_op jit(solution)/shard_map/all_gather | solution.py:79
  216.6 11.4 %copy.18 = bf16[512,8,1024]{0,2,1:T(8,128)(2,1)} copy(bf16[512,8,1024]{2,0,1:T(8,128)(2,1)} %bitcast.36) | data formatting | bytes 16777216 | tf_op jit(solution)/shard_map/reshape | solution.py:79
  228.0 100.7 %all-gather.4.cloned.1.call-done = bf16[8192,1024]{1,0:T(8,128)(2,1)} async-done(((bf16[512,1024]{1,0:T(8,128)(2,1)}), bf16[8192,1024]{1,0:T(8,128)(2,1)}) %all-gather.4.cloned.1.call-update) | async-done | bytes 16777232 | tf_op jit(solution)/shard_map/all_gather | solution.py:87
  328.7 0.2 mul.47
  328.9 14.9 %fusion.14 = (f32[1024]{0:T(1024)S(1)}, f32[512,1024]{1,0:T(8,128)S(1)}) fusion(f32[64,8,8,128]{3,2,1,0:T(8,128)S(1)} %bitcast.40, bf16[512,8192]{0,1:T(8,128)(2,1)} %bitcast.37, bf16[8192,1024]{1,0:T(8,128)(2,1)} %all-gather.4.cloned.1.call-done), kind=kOutput, calls=%fused_computation.43 | convolution fusion | flops 8591506432 | bytes 29364224 | tf_op jit(solution)/shard_map/dot_general | solution.py:85
  343.8 33.8 %psum.15 = f32[1024]{0:T(1024)S(1)} all-reduce(f32[1024]{0:T(1024)S(1)} %get-tuple-element.5), channel_id=1, replica_groups=mesh['row'=16,'col'=8] {'row'}, use_global_device_ids=true, to_apply=%region_4.5 | all-reduce | flops 1024 | bytes 8192 | tf_op jit(solution)/shard_map/psum | solution.py:91
  377.6 0.3 divide_bitcast_fusion
  377.9 0.5 copy.28
  378.4 1.9 fusion.5
  380.3 3.3 copy.19
  383.6 5.3 %all-to-all-start = ((f32[16,512,128]{2,1,0:T(8,128)}), f32[16,512,128]{2,1,0:T(8,128)}, u32[]{:S(2)}, u32[]{:S(2)}) async-start(f32[16,512,128]{2,1,0:T(8,128)} %copy.19), calls=%async_computation | async-start | bytes 8388608 | tf_op jit(solution)/shard_map/all_to_all | solution.py:93
  388.9 0.1 eq.99
  389.0 0.1 select_reduce_fusion.1
  389.1 0.1 broadcast_compare_fusion
  389.2 0.4 select_reduce_fusion
  389.6 0.1 copy.21
  389.6 47.6 %all-to-all-done = f32[16,512,128]{2,1,0:T(8,128)} async-done(((f32[16,512,128]{2,1,0:T(8,128)}), f32[16,512,128]{2,1,0:T(8,128)}, u32[]{:S(2)}, u32[]{:S(2)}) %all-to-all-start) | async-done | bytes 4194336 | tf_op jit(solution)/shard_map/all_to_all | solution.py:93
  437.2 6.8 %fusion = f32[512,128,8]{1,2,0:T(8,128)S(1)} fusion(f32[8,16,1]{0,1,2:T(8,128)S(1)} %bitcast.41, f32[16,512,128]{2,1,0:T(8,128)} %all-to-all-done), kind=kOutput, calls=%fused_computation | convolution fusion | flops 100663296 | bytes 6291968 | tf_op jit(solution)/shard_map/sp,prb->rsb/dot_general | solution.py:54
  444.1 1.8 copy.40
  (6 shorter events, 0.0 us)
Async XLA Ops:
  6.5 210.0 %all-gather.6.cloned.1.call-start = ((), (), s32[]{:S(2)}) async-start(), calls=%async_computation.2 | async-start | bytes 9437184 | tf_op jit(solution)/shard_map/all_gather | solution.py:79
  6.5 1.6 copy-start
  50.2 0.8 copy-start.1
  50.3 278.4 %all-gather.4.cloned.1.call-start = ((), (), s32[]{:S(2)}) async-start(), calls=%async_computation.1 | async-start | bytes 17825792 | tf_op jit(solution)/shard_map/all_gather | solution.py:87
  383.6 53.7 %all-to-all-start = ((f32[16,512,128]{2,1,0:T(8,128)}), f32[16,512,128]{2,1,0:T(8,128)}, u32[]{:S(2)}, u32[]{:S(2)}) async-start(f32[16,512,128]{2,1,0:T(8,128)} %copy.19), calls=%async_computation | async-start | bytes 8388608 | tf_op jit(solution)/shard_map/all_to_all | solution.py:93
Sparse Core Ops, SparseCore 0:
  50.4 166.1 all-gather.5
  219.0 109.6 all-gather.3
